TPU v7x, 32 devices: a whole 2x2x4 slice. The times are simulated.
32 devices in a mesh: groups: 2 (over x), dp: 2 (over core), tensor: 8 (over z, y).
Axes of the slice: x: 2, y: 2, z: 4, core: 2. Of those that a mesh axis runs over, the one named last changes fastest.
Arguments:
- hidden: bfloat16 [4, 1024, 8192], P(('groups', 'dp'), 'tensor'), parts along dimension 0, may hold values from -24 to 24
- query_weight: bfloat16 [8192, 4096], P(None, 'tensor'), may hold values from -0.0625 to 0.0625
- key_weight: bfloat16 [8, 4096, 128], P('tensor'), may hold values from -0.0625 to 0.0625
- value_weight: bfloat16 [8, 4096, 128], P('tensor'), may hold values from -0.0625 to 0.0625
- head_grad: bfloat16 [4, 1024, 4096], P(('groups', 'dp'), None, 'tensor'), parts along dimension 0, may hold values from -6 to 6
- lengths: int32 [4], P(('groups', 'dp')), parts along dimension 0, may hold values from 256 to 1024, as said below
Outputs:
- fisher_key: float32 [16, 4096, 128], P(('groups', 'tensor'), 'dp'), parts along dimension 0
- fisher_value: float32 [16, 4096, 128], P(('groups', 'tensor'), 'dp'), parts along dimension 0
There are 2 independent parts, one for each index of `groups`. A program takes and returns all parts, laid end to end along the dimension named above; an argument that names none is the same for every part. Nothing has to cross between parts.
Inputs may be any that keep to these rules, and one draw needn't show every extreme that they name: `lengths`: some sequence of each part has length 1024.
All inputs are finite; a program needn't handle non-finite values.
Results may differ from a plain program's by a relative error of at most 0.013.
The roundings to bfloat16 on the way count: a program that leaves them out, or rounds other values in their place, can miss the bound.
Values may be sent and summed in bfloat16 or wider, within the bound.
A program may use at most 256 MiB of HBM per device.

v0:
```python
import math
import jax
import jax.numpy as jnp
from jax import lax
from jax.sharding import PartitionSpec as P

rope_base = 1000000.0
far_below = -1e30


def from_partner(value, axis, stride):
    mask = 2**stride
    pairs = [(source, source ^ mask) for source in range(lax.axis_size(axis))]
    return lax.ppermute(value, axis, pairs)


def angle_table(length, head_width):
    position = jnp.arange(length, dtype=jnp.float32)[:, None]
    frequency = rope_base ** (-2.0 * jnp.arange(head_width // 2, dtype=jnp.float32) / head_width)
    return (position * frequency)[:, None, :]


def rotate(vectors, angles):
    half_dim = vectors.shape[-1] // 2
    lead_half = vectors[..., :half_dim]
    tail_half = vectors[..., half_dim:]
    cosine = jnp.cos(angles)
    sines = jnp.sin(angles)
    return jnp.concatenate(
        [lead_half * cosine - tail_half * sines, tail_half * cosine + lead_half * sines], axis=-1
    )


def unrotate(vectors, angles):
    half_dim = vectors.shape[-1] // 2
    lead_half = vectors[..., :half_dim]
    tail_half = vectors[..., half_dim:]
    cosine = jnp.cos(angles)
    sines = jnp.sin(angles)
    return jnp.concatenate(
        [lead_half * cosine + tail_half * sines, tail_half * cosine - lead_half * sines], axis=-1
    )


def local(hidden, query_weight, key_weight, value_weight, head_grad, lengths):
    seq_count, tok_rows, model_width = hidden.shape
    length = tok_rows * lax.axis_size("tensor")
    half_width = model_width // 2
    head_width = key_weight.shape[2]
    heads_here = query_weight.shape[1] // head_width
    query_cols = heads_here * head_width
    pair_side = lax.axis_index("tensor") % 2
    score_scale = 1.0 / math.sqrt(head_width)
    angles = angle_table(length, head_width)
    pair_rows = jnp.concatenate([key_weight[0], value_weight[0]], axis=1)
    collected_rows = lax.all_gather(hidden, "tensor", axis=1, tiled=True)
    query_part = jnp.dot(collected_rows, query_weight, preferred_element_type=jnp.float32)
    own_part = lax.dynamic_slice_in_dim(collected_rows, pair_side * half_width, half_width, 2)
    kv_part = jnp.dot(own_part, pair_rows, preferred_element_type=jnp.float32)
    projected = jnp.concatenate([query_part, kv_part], axis=-1)
    kv_mixed = projected[..., query_cols:]
    kv_mixed = kv_mixed + from_partner(kv_mixed, "tensor", 0)
    queries = rotate(
        projected[..., :query_cols].reshape(seq_count, length, heads_here, head_width), angles
    ).astype(jnp.bfloat16)
    keys = rotate(kv_mixed[..., :head_width][:, :, None, :], angles)[:, :, 0, :].astype(
        jnp.bfloat16
    )
    values = kv_mixed[..., head_width:].astype(jnp.bfloat16)
    live_rows = jnp.arange(length, dtype=jnp.int32)[None, :] < lengths[:, None]
    upstream = jnp.where(live_rows[:, :, None], head_grad, jnp.zeros_like(head_grad)).reshape(
        seq_count, length, heads_here, head_width
    )
    block_rows = 512
    block_count = length // block_rows
    kv_accum = jnp.zeros((seq_count, length, 2 * head_width), jnp.float32)
    for block_idx in range(block_count):
        row_begin = block_idx * block_rows
        row_end = row_begin + block_rows
        query_block = queries[:, row_begin:row_end]
        up_block = upstream[:, row_begin:row_end]
        key_tile_block = keys[:, :row_end]
        value_block = values[:, :row_end]
        scores = (
            jnp.einsum(
                "sqhd,skd->shqk", query_block, key_tile_block, preferred_element_type=jnp.float32
            )
            * score_scale
        )
        causal_ok = (row_begin + jnp.arange(block_rows))[:, None] >= jnp.arange(row_end)[None, :]
        scores = jnp.where(causal_ok, scores, far_below)
        exp_scores = jnp.exp(scores - jnp.max(scores, axis=-1, keepdims=True))
        prob_rows = exp_scores / jnp.sum(exp_scores, axis=-1, keepdims=True)
        dprob = jnp.einsum(
            "sqhd,skd->shqk", up_block, value_block, preferred_element_type=jnp.float32
        )
        row_dot = jnp.sum(prob_rows * dprob, axis=-1, keepdims=True)
        dscore = (prob_rows * (dprob - row_dot) * score_scale).astype(jnp.bfloat16)
        key_portion = jnp.einsum(
            "shqk,sqhd->skd", dscore, query_block, preferred_element_type=jnp.float32
        )
        value_part = jnp.einsum(
            "shqk,sqhd->skd",
            prob_rows.astype(jnp.bfloat16),
            up_block,
            preferred_element_type=jnp.float32,
        )
        block_grad = jnp.concatenate([key_portion, value_part], axis=-1)
        kv_accum = kv_accum + jnp.pad(block_grad, ((0, 0), (0, length - row_end), (0, 0)))
    kv_accum = kv_accum + from_partner(kv_accum, "tensor", 0)
    key_gradient = unrotate(kv_accum[..., :head_width][:, :, None, :], angles)[:, :, 0, :]
    key_value_gradient = jnp.concatenate(
        [key_gradient, kv_accum[..., head_width:]], axis=-1
    ).astype(jnp.bfloat16)
    owned_columns = lax.dynamic_slice_in_dim(collected_rows, pair_side * half_width, half_width, 2)
    sample_count = jnp.einsum(
        "jyv,jyo->jvo", owned_columns, key_value_gradient, preferred_element_type=jnp.float32
    )
    squares = jnp.sum(sample_count * sample_count, axis=0)
    fisher_key, fisher_value = (
        lax.psum_scatter(squares[:, :head_width], "dp", scatter_dimension=0, tiled=True),
        lax.psum_scatter(squares[:, head_width:], "dp", scatter_dimension=0, tiled=True),
    )
    return (fisher_key[None], fisher_value[None])


def solution(mesh):
    in_specs = (
        P(("groups", "dp"), "tensor", None),
        P(None, "tensor"),
        P("tensor", None, None),
        P("tensor", None, None),
        P(("groups", "dp"), None, "tensor"),
        P(("groups", "dp")),
    )
    out_specs = (P(("groups", "tensor"), "dp", None), P(("groups", "tensor"), "dp", None))
    return jax.shard_map(local, mesh=mesh, in_specs=in_specs, out_specs=out_specs, check_vma=False)
```

profile of v0, /device:TPU:0, one launch (start us, length us, event | category | flops | bytes accessed | tf_op | source)
XLA Modules:
  0.0 360.1 jit_solution(1559386330099793040)
XLA Ops:
  7.2 0.0 all-gather.2.cloned.1.call-start
  7.2 0.7 all-gather.2.cloned.1.call-update
  7.9 0.0 reduce-scatter.3.cloned.1.call-start
  8.0 0.0 copy-start
  8.0 11.4 %copy.50 = bf16[512,8192]{1,0:T(8,128)(2,1)} copy(bf16[512,8192]{0,1:T(8,128)(2,1)} %bitcast.207) | data formatting | bytes 16777216 | tf_op jit(solution)/shard_map/dot_general | solution.py:57
  19.3 0.0 copy-done
  19.3 0.5 copy.24
  20.6 0.1 iota_compare_fusion.2
  20.7 1.0 fusion.80
  21.7 0.4 iota_compare_fusion
  22.0 0.1 broadcast_select_fusion
  22.1 218.3 %all-gather.2.cloned.1.call-done = bf16[1,1024,8192]{2,1,0:T(8,128)(2,1)} async-done(((bf16[1,128,8192]{2,1,0:T(8,128)(2,1)}), bf16[1,1024,8192]{2,1,0:T(8,128)(2,1)}) %all-gather.2.cloned.1.call-update) | async-done | bytes 16777232 | tf_op jit(solution)/shard_map/all_gather | solution.py:56
  240.5 6.3 %fusion.49 = f32[1,1024,256]{1,2,0:T(8,128)S(1)} fusion(bf16[4096,128]{1,0:T(8,128)(2,1)} %bitcast.215, bf16[4096,128]{1,0:T(8,128)(2,1)} %bitcast.216, bf16[1,1024,8192]{2,1,0:T(8,128)(2,1)} %all-gather.2.cloned.1.call-done, s32[]{:T(128)S(6)} %select_n.24), kind=kOutput, calls=%fused_computation.48 | convolution fusion | flops 2151677952 | bytes 11534340 | tf_op jit(solution)/shard_map/dot_general | solution.py:59
  246.8 0.6 collective-permute-start
  247.4 14.4 %fusion.44 = f32[1,1024,4,128]{1,3,2,0:T(8,128)S(1)} fusion(bf16[4,128,8192]{2,1,0:T(8,128)(2,1)} %bitcast.208, bf16[1,1024,8192]{2,1,0:T(8,128)(2,1)} %all-gather.2.cloned.1.call-done), kind=kOutput, calls=%fused_computation.47 | convolution fusion | flops 8589934592 | bytes 27262976 | tf_op jit(solution)/shard_map/dot_general | solution.py:57
  261.8 0.4 add_convert_fusion
  262.1 9.2 %collective-permute-done = f32[1,1024,256]{1,2,0:T(8,128)S(1)} collective-permute-done((f32[1,1024,256]{1,2,0:T(8,128)S(1)}, f32[1,1024,256]{1,2,0:T(8,128)S(1)}, u32[]{:S(2)}, u32[]{:S(2)}) %collective-permute-start) | collective-permute-done | bytes 1048608 | tf_op jit(solution)/shard_map/ppermute | solution.py:14
  271.3 0.2 fusion.102
  271.6 1.2 subtract_convert_fusion.2
  272.8 1.7 fusion.14
  274.5 2.0 fusion.11
  276.5 2.7 fusion.54
  279.3 5.0 %fusion.2 = (f32[4,512]{1,0:T(4,128)S(1)}, f32[1024,512,4]{1,0,2:T(8,128)}) fusion(f32[4,512]{1,0:T(4,128)S(1)} %fusion.11, f32[4,512]{1,0:T(4,128)S(1)} %get-tuple-element.18, f32[1024,512,4]{1,0,2:T(8,128)S(1)} %get-tuple-element.19, pred[512,1024]{0,1:T(8,128)(4,1)S(1)} %iota_compare_fusion, bf16[1,1024,4,128]{1,3,2,0:T(8,128)(2,1)S(1)} %bitcast.210, ...), kind=kOutput, calls=%fused_computation.5 | convolution fusion | flops 549451776 | bytes 18112512 | tf_op jit(solution)/shard_map/sqhd,skd->shqk/dot_general | solution.py:94
  284.3 0.9 fusion.30
  285.2 0.9 fusion.29
  286.1 1.7 fusion.21
  287.8 1.4 fusion.60
  289.2 6.2 %fusion.57 = f32[1,1024,128]{1,2,0:T(8,128)S(1)} fusion(f32[1024,512,4]{1,0,2:T(8,128)} %get-tuple-element.21, f32[4,512]{1,0:T(4,128)S(1)} %get-tuple-element.20, f32[4,512]{1,0:T(4,128)S(1)} %fusion.11, f32[4,512]{1,0:T(4,128)S(1)} %get-tuple-element.18, f32[1024,512,4]{1,0,2:T(8,128)S(1)} %get-tuple-element.19, ...), kind=kOutput, calls=%fused_computation.50 | convolution fusion | flops 554696704 | bytes 18898944 | tf_op jit(solution)/shard_map/shqk,sqhd->skd/dot_general | solution.py:99
  295.4 1.8 fusion.63
  297.2 0.1 fusion.66
  297.4 0.6 collective-permute-start.1
  298.0 23.0 %collective-permute-done.1 = f32[1,1024,256]{1,2,0:T(8,128)S(1)} collective-permute-done((f32[1,1024,256]{1,2,0:T(8,128)S(1)}, f32[1,1024,256]{1,2,0:T(8,128)S(1)}, u32[]{:S(2)}, u32[]{:S(2)}) %collective-permute-start.1) | collective-permute-done | bytes 1048608 | tf_op jit(solution)/shard_map/ppermute | solution.py:14
  321.0 0.2 add.50
  321.3 1.2 add_convert_fusion.1
  322.5 6.0 %fusion.15 = f32[4096,256]{1,0:T(8,128)S(1)} fusion(bf16[1,1024,8192]{2,1,0:T(8,128)(2,1)} %all-gather.2.cloned.1.call-done, s32[]{:T(128)S(6)} %select_n.24, bf16[1024,128]{0,1:T(8,128)(2,1)S(1)} %fusion.75, bf16[1024,128]{0,1:T(8,128)(2,1)S(1)} %maximum_bitcast_fusion.3), kind=kOutput, calls=%fused_computation.19 | convolution fusion | flops 2149580800 | bytes 13107204 | tf_op jit(solution)/shard_map/jyv,jyo->jvo/dot_general | solution.py:116
  328.5 2.2 fusion.103
  330.7 0.0 reduce-scatter.3.cloned.1.call-update
  330.7 0.0 reduce-scatter.5.cloned.1.call-start
  330.7 0.7 reduce-scatter.5.cloned.1.call-update
  331.4 8.4 %reduce-scatter.3.cloned.1.call-done = f32[2048,128]{1,0:T(8,128)} async-done(((f32[4096,128]{1,0:T(8,128)}), f32[2048,128]{1,0:T(8,128)}) %reduce-scatter.3.cloned.1.call-update) | async-done | bytes 1048592 | tf_op jit(solution)/shard_map/reduce_scatter | solution.py:121
  339.9 13.7 %reduce-scatter.5.cloned.1.call-done = f32[2048,128]{1,0:T(8,128)} async-done(((f32[4096,128]{1,0:T(8,128)}), f32[2048,128]{1,0:T(8,128)}) %reduce-scatter.5.cloned.1.call-update) | async-done | bytes 1048592 | tf_op jit(solution)/shard_map/reduce_scatter | solution.py:122
  (8 shorter events, 0.2 us)
Async XLA Ops:
  7.2 233.3 %all-gather.2.cloned.1.call-start = ((), (), s32[]{:S(2)}) async-start(), calls=%async_computation.2 | async-start | bytes 18874368 | tf_op jit(solution)/shard_map/all_gather | solution.py:56
  7.9 332.0 %reduce-scatter.3.cloned.1.call-start = ((), (), s32[]{:S(2)}) async-start(), calls=%async_computation.3 | async-start | bytes 3145728 | tf_op jit(solution)/shard_map/reduce_scatter | solution.py:121
  8.0 11.4 %copy-start = (bf16[1,1024,512]{2,1,0:T(8,128)(2,1)S(1)}, bf16[1,1024,512]{2,1,0:T(8,128)(2,1)}, u32[]{:S(2)}) copy-start(bf16[1,1024,512]{2,1,0:T(8,128)(2,1)} %param.10) | copy-start | bytes 3145732
  246.8 24.6 %collective-permute-start = (f32[1,1024,256]{1,2,0:T(8,128)S(1)}, f32[1,1024,256]{1,2,0:T(8,128)S(1)}, u32[]{:S(2)}, u32[]{:S(2)}) collective-permute-start(f32[1,1024,256]{1,2,0:T(8,128)S(1)} %fusion.49), channel_id=1, source_target_pairs={{0,1},{1,0},{2,3},{3,2},{4,5},{5,4},{6,7},{7,6},{8,9},{9,8},{10,11... | collective-permute-start | bytes 3145736 | tf_op jit(solution)/shard_map/ppermute | solution.py:14
  297.4 23.6 %collective-permute-start.1 = (f32[1,1024,256]{1,2,0:T(8,128)S(1)}, f32[1,1024,256]{1,2,0:T(8,128)S(1)}, u32[]{:S(2)}, u32[]{:S(2)}) collective-permute-start(f32[1,1024,256]{1,2,0:T(8,128)S(1)} %fusion.66), channel_id=1, source_target_pairs={{0,1},{1,0},{2,3},{3,2},{4,5},{5,4},{6,7},{7,6},{8,9},{9,8},{10,11... | collective-permute-start | bytes 3145736 | tf_op jit(solution)/shard_map/ppermute | solution.py:14
  330.7 22.9 %reduce-scatter.5.cloned.1.call-start = ((), (), s32[]{:S(2)}) async-start(), calls=%async_computation.4 | async-start | bytes 3145728 | tf_op jit(solution)/shard_map/reduce_scatter | solution.py:122
Sparse Core Ops, SparseCore 0:
  10.1 230.3 all-gather.1
  330.8 9.0 reduce-scatter.2
  342.8 10.7 reduce-scatter.4
where the time goes:
time: 361 us; the launch traced here: 360 us
  waiting for transfers between devices  274 us (76%)
  matrix products  48.1 us (13%)
  between operations  14.6 us (4%)
  local copies, waits for them, and re-layouts  14.2 us (4%)
  other arithmetic  7.71 us (2%)
    all_gather x1, waiting for transfers between devices, local(): collected_rows = lax.all_gather(hidden, 'tensor', axis=1, tiled=True)  218 us
    ppermute x2, waiting for transfers between devices, from_partner(): return lax.ppermute(value, axis, pairs)  32.2 us
    dot_general x1, matrix products, local(): jnp.dot(collected_rows, query_weight, preferred_element_type=jnp.float32)  14.4 us
    reduce_scatter x1, waiting for transfers between devices, local(): lax.psum_scatter(squares[:, head_width:], 'dp', scatter_dimension=0, tile...  13.7 us
    dot_general x1, local copies, waits for them, and re-layouts, local(): jnp.dot(collected_rows, query_weight, preferred_element_type=jnp.float32)  11.4 us
    reduce_scatter x1, waiting for transfers between devices, local(): lax.psum_scatter(squares[:, :head_width], 'dp', scatter_dimension=0, tile...  8.45 us
    dot_general x2, matrix products, local(): jnp.einsum('shqk,sqhd->skd', dscore, query_block, preferred_element_type=...  8.03 us
  transfers between devices with their start and end apart: 5, of which 5 were waited for; matrix products, arithmetic and copies ran while one was open for 8% of the time, Pallas kernels for 0%

commit v1 on v0

--- a/solution.py
+++ b/solution.py
@@ -53,7 +53,36 @@
     score_scale = 1.0 / math.sqrt(head_width)
     angles = angle_table(length, head_width)
     pair_rows = jnp.concatenate([key_weight[0], value_weight[0]], axis=1)
-    collected_rows = lax.all_gather(hidden, "tensor", axis=1, tiled=True)
+    state_now = lax.axis_size("tensor")
+    b_next, part_next, mixed_arr = (state_now, lax.axis_index("tensor"), hidden.shape[1])
+    items = []
+    for j, idx in enumerate(hidden.shape):
+        items.append(idx * b_next if j == 1 else idx)
+    main = jnp.zeros(items, hidden.dtype)
+    side_arr = work_now = hidden
+    ii = 1
+    collected_rows = lax.dynamic_update_slice_in_dim(main, hidden, part_next * mixed_arr, axis=1)
+    while ii < b_next // 2 + 1:
+        stack_in = []
+        j = 0
+        while j < b_next:
+            stack_in.append((j, (j + 1) % b_next))
+            j += 1
+        side_arr = lax.ppermute(side_arr, "tensor", stack_in)
+        collected_rows = lax.dynamic_update_slice_in_dim(
+            collected_rows, side_arr, (part_next - ii) % b_next * mixed_arr, axis=1
+        )
+        if 2 * ii < b_next:
+            all_rows = []
+            j = 0
+            while j < b_next:
+                all_rows.append((j, (j - 1) % b_next))
+                j += 1
+            work_now = lax.ppermute(work_now, "tensor", all_rows)
+            collected_rows = lax.dynamic_update_slice_in_dim(
+                collected_rows, work_now, (part_next + ii) % b_next * mixed_arr, axis=1
+            )
+        ii += 1
     query_part = jnp.dot(collected_rows, query_weight, preferred_element_type=jnp.float32)
     own_part = lax.dynamic_slice_in_dim(collected_rows, pair_side * half_width, half_width, 2)
     kv_part = jnp.dot(own_part, pair_rows, preferred_element_type=jnp.float32)

time: 361 us -> 453 us (1.25)
  waiting for transfers between devices: 274 us -> 338 us
  starting transfers between devices: 1.35 us -> 20.3 us
  local copies, waits for them, and re-layouts: 14.2 us -> 23.8 us
    ppermute x0 -> x7, waiting for transfers between devices: none -> 281 us  [the longest x4 236 us: local(): side_arr = lax.ppermute(side_arr, 'tensor', stack_in)]
    all_gather x1 -> x0, waiting for transfers between devices: 218 us -> none  [local(): collected_rows = lax.all_gather(hidden, 'tensor', axis=1, tiled=True)]
    ppermute x0 -> x7, starting transfers between devices: none -> 19.8 us  [the longest x4 10.4 us: local(): side_arr = lax.ppermute(side_arr, 'tensor', stack_in)]
    dynamic_update_slice x0 -> x8, local copies, waits for them, and re-layouts: none -> 6.77 us  [the longest x4 4.18 us: local(): lax.dynamic_update_slice_in_dim(collected_rows, side_arr, (part_next - ii...]
  transfers between devices with their start and end apart: 5 -> 11, of which waited for: 5 -> 8; matrix products, arithmetic and copies ran while one was open for 8% -> 8% of each run, Pallas kernels for 0% -> 0%
where the time goes in v1:
time: 453 us; the launch traced here: 452 us
  waiting for transfers between devices  338 us (75%)
  matrix products  44.7 us (10%)
  local copies, waits for them, and re-layouts  23.8 us (5%)
  starting transfers between devices  20.3 us (4%)
  between operations  15.1 us (3%)
  other arithmetic  9.94 us (2%)
    ppermute x4, waiting for transfers between devices, local(): side_arr = lax.ppermute(side_arr, 'tensor', stack_in)  236 us
    ppermute x3, waiting for transfers between devices, local(): work_now = lax.ppermute(work_now, 'tensor', all_rows)  45.5 us
    ppermute x2, waiting for transfers between devices, from_partner(): return lax.ppermute(value, axis, pairs)  36.3 us
    reduce_scatter x1, waiting for transfers between devices, local(): lax.psum_scatter(squares[:, head_width:], 'dp', scatter_dimension=0, tile...  13.7 us
    dot_general x1, matrix products, local(): jnp.dot(collected_rows, query_weight, preferred_element_type=jnp.float32)  12.5 us
    dot_general x2, matrix products, local(): jnp.einsum('shqk,sqhd->skd', dscore, query_block, preferred_element_type=...  11.7 us
    dot_general x1, local copies, waits for them, and re-layouts, local(): jnp.dot(collected_rows, query_weight, preferred_element_type=jnp.float32)  11.6 us
    ppermute x4, starting transfers between devices, local(): side_arr = lax.ppermute(side_arr, 'tensor', stack_in)  10.4 us
  transfers between devices with their start and end apart: 11, of which 8 were waited for; matrix products, arithmetic and copies ran while one was open for 8% of the time, Pallas kernels for 0%

profile of v1, /device:TPU:0, one launch (start us, length us, event | category | flops | bytes accessed | tf_op | source)
XLA Modules:
  0.0 451.9 jit_solution(17496174831746953312)
XLA Ops:
  7.2 3.0 collective-permute-start
  10.2 3.1 collective-permute-start.1
  13.3 87.0 %collective-permute-done = bf16[1,128,8192]{2,1,0:T(8,128)(2,1)} collective-permute-done((bf16[1,128,8192]{2,1,0:T(8,128)(2,1)}, bf16[1,128,8192]{2,1,0:T(8,128)(2,1)}, u32[]{:S(2)}, u32[]{:S(2)}) %collective-permute-start) | collective-permute-done | bytes 2097184 | tf_op jit(solution)/shard_map/ppermute | solution.py:71
  100.4 2.5 collective-permute-start.2
  102.9 11.6 %copy.50 = bf16[512,8192]{1,0:T(8,128)(2,1)} copy(bf16[512,8192]{0,1:T(8,128)(2,1)} %bitcast.207) | data formatting | bytes 16777216 | tf_op jit(solution)/shard_map/dot_general | solution.py:86
  114.5 0.5 copy.24
  115.8 0.4 iota_compare_fusion
  116.2 1.0 broadcast_select_fusion
  117.3 1.6 broadcast_in_dim.34
  118.9 0.3 constant_dynamic-update-slice_fusion.7
  119.2 3.2 collective-permute-start.3
  122.4 1.0 fusion.80
  123.4 68.7 %collective-permute-done.2 = bf16[1,128,8192]{2,1,0:T(8,128)(2,1)} collective-permute-done((bf16[1,128,8192]{2,1,0:T(8,128)(2,1)}, bf16[1,128,8192]{2,1,0:T(8,128)(2,1)}, u32[]{:S(2)}, u32[]{:S(2)}) %collective-permute-start.2) | collective-permute-done | bytes 2097184 | tf_op jit(solution)/shard_map/ppermute | solution.py:71
  192.1 2.5 collective-permute-start.4
  194.6 1.8 constant_dynamic-update-slice_fusion.6
  196.5 1.8 constant_dynamic-update-slice_fusion.5
  198.3 3.1 collective-permute-start.5
  201.4 1.8 constant_dynamic-update-slice_fusion.4
  203.3 79.9 %collective-permute-done.4 = bf16[1,128,8192]{2,1,0:T(8,128)(2,1)S(1)} collective-permute-done((bf16[1,128,8192]{2,1,0:T(8,128)(2,1)}, bf16[1,128,8192]{2,1,0:T(8,128)(2,1)S(1)}, u32[]{:S(2)}, u32[]{:S(2)}) %collective-permute-start.4) | collective-permute-done | bytes 2097184 | tf_op jit(solution)/shard_map/ppermute | solution.py:71
  283.2 2.4 collective-permute-start.6
  285.8 0.2 constant_dynamic-update-slice_fusion.2
  286.1 45.5 %collective-permute-done.5 = bf16[1,128,8192]{2,1,0:T(8,128)(2,1)S(1)} collective-permute-done((bf16[1,128,8192]{2,1,0:T(8,128)(2,1)S(1)}, bf16[1,128,8192]{2,1,0:T(8,128)(2,1)S(1)}, u32[]{:S(2)}, u32[]{:S(2)}) %collective-permute-start.5) | collective-permute-done | bytes 2097184 | tf_op jit(solution)/shard_map/ppermute | solution.py:81
  331.8 0.2 constant_dynamic-update-slice_fusion
  332.1 0.7 copy-done.5
  332.8 2.4 fusion.49
  335.3 12.5 %fusion.44 = f32[1,1024,4,128]{1,3,2,0:T(8,128)S(1)} fusion(bf16[4,128,8192]{2,1,0:T(8,128)(2,1)} %bitcast.208, bf16[1,1024,8192]{2,1,0:T(8,128)(2,1)S(1)} %constant_dynamic-update-slice_fusion), kind=kOutput, calls=%fused_computation.47 | convolution fusion | flops 8589934592 | bytes 27262976 | tf_op jit(solution)/shard_map/dot_general | solution.py:86
  347.8 0.4 add_convert_fusion
  348.1 12.3 %collective-permute-done.7 = f32[1,1024,256]{1,2,0:T(8,128)} collective-permute-done((f32[1,1024,256]{1,2,0:T(8,128)S(1)}, f32[1,1024,256]{1,2,0:T(8,128)}, u32[]{:S(2)}, u32[]{:S(2)}) %collective-permute-start.7) | collective-permute-done | bytes 1048608 | tf_op jit(solution)/shard_map/ppermute | solution.py:14
  360.5 1.4 fusion.102
  361.9 1.2 subtract_convert_fusion.2
  363.1 1.7 fusion.14
  364.8 1.8 fusion.11
  366.8 2.7 fusion.54
  369.6 5.2 %fusion.2 = (f32[4,512]{1,0:T(4,128)S(1)}, f32[1024,512,4]{1,0,2:T(8,128)}) fusion(f32[4,512]{1,0:T(4,128)S(1)} %fusion.11, f32[4,512]{1,0:T(4,128)S(1)} %get-tuple-element.18, f32[1024,512,4]{1,0,2:T(8,128)S(1)} %get-tuple-element.19, pred[512,1024]{0,1:T(8,128)(4,1)S(1)} %iota_compare_fusion, bf16[1,1024,4,128]{1,3,2,0:T(8,128)(2,1)S(1)} %bitcast.210, ...), kind=kOutput, calls=%fused_computation.5 | convolution fusion | flops 549451776 | bytes 18112512 | tf_op jit(solution)/shard_map/sqhd,skd->shqk/dot_general | solution.py:123
  374.8 0.9 fusion.30
  375.7 0.9 fusion.29
  376.6 3.5 fusion.21
  380.1 1.4 fusion.60
  381.5 7.7 %fusion.57 = f32[1,1024,128]{1,2,0:T(8,128)S(1)} fusion(f32[1024,512,4]{1,0,2:T(8,128)} %get-tuple-element.21, f32[4,512]{1,0:T(4,128)S(1)} %get-tuple-element.20, f32[4,512]{1,0:T(4,128)S(1)} %fusion.11, f32[4,512]{1,0:T(4,128)S(1)} %get-tuple-element.18, f32[1024,512,4]{1,0,2:T(8,128)} %copy-done, pred[512,1024]{0,1:T(8,128)(4,1)S(1)} %iota_compare_fusion, ...), kind=kOutput, calls=%fused_computation.50 | convolution fusion | flops 554696704 | bytes 18898944 | tf_op jit(solution)/shard_map/shqk,sqhd->skd/dot_general | solution.py:128
  389.2 4.1 fusion.63
  393.4 0.3 collective-permute-start.8
  393.7 24.0 %collective-permute-done.8 = f32[1,1024,256]{1,2,0:T(8,128)S(1)} collective-permute-done((f32[1,1024,256]{1,2,0:T(8,128)S(1)}, f32[1,1024,256]{1,2,0:T(8,128)S(1)}, u32[]{:S(2)}, u32[]{:S(2)}) %collective-permute-start.8) | collective-permute-done | bytes 1048608 | tf_op jit(solution)/shard_map/ppermute | solution.py:14
  417.9 1.4 add_convert_fusion.1
  419.4 2.7 fusion.15
  422.1 2.2 fusion.103
  424.4 0.7 reduce-scatter.5.cloned.1.call-update
  425.1 6.3 %reduce-scatter.3.cloned.1.call-done = f32[2048,128]{1,0:T(8,128)} async-done(((f32[4096,128]{1,0:T(8,128)}), f32[2048,128]{1,0:T(8,128)}) %reduce-scatter.3.cloned.1.call-update) | async-done | bytes 1048592 | tf_op jit(solution)/shard_map/reduce_scatter | solution.py:150
  431.4 13.7 %reduce-scatter.5.cloned.1.call-done = f32[2048,128]{1,0:T(8,128)} async-done(((f32[4096,128]{1,0:T(8,128)}), f32[2048,128]{1,0:T(8,128)}) %reduce-scatter.5.cloned.1.call-update) | async-done | bytes 1048592 | tf_op jit(solution)/shard_map/reduce_scatter | solution.py:151
  (31 shorter events, 1.3 us)
Async XLA Ops:
  7.2 424.2 %reduce-scatter.3.cloned.1.call-start = ((), (), s32[]{:S(2)}) async-start(), calls=%async_computation.2 | async-start | bytes 3145728 | tf_op jit(solution)/shard_map/reduce_scatter | solution.py:150
  7.2 93.2 %collective-permute-start = (bf16[1,128,8192]{2,1,0:T(8,128)(2,1)}, bf16[1,128,8192]{2,1,0:T(8,128)(2,1)}, u32[]{:S(2)}, u32[]{:S(2)}) collective-permute-start(bf16[1,128,8192]{2,1,0:T(8,128)(2,1)} %param.6), channel_id=1, source_target_pairs={{0,1},{1,2},{2,3},{3,4},{4,5},{5,6},{6,7},{7,0},{8,9},{9,10},{10,1... | collective-permute-start | bytes 6291464 | tf_op jit(solution)/shard_map/ppermute | solution.py:71
  10.2 109.0 %collective-permute-start.1 = (bf16[1,128,8192]{2,1,0:T(8,128)(2,1)}, bf16[1,128,8192]{2,1,0:T(8,128)(2,1)}, u32[]{:S(2)}, u32[]{:S(2)}) collective-permute-start(bf16[1,128,8192]{2,1,0:T(8,128)(2,1)} %param.6), channel_id=1, source_target_pairs={{0,7},{1,0},{2,1},{3,2},{4,3},{5,4},{6,5},{7,6},{8,15},{9,8},{10,9... | collective-permute-start | bytes 6291464 | tf_op jit(solution)/shard_map/ppermute | solution.py:81
  100.4 91.8 %collective-permute-start.2 = (bf16[1,128,8192]{2,1,0:T(8,128)(2,1)}, bf16[1,128,8192]{2,1,0:T(8,128)(2,1)}, u32[]{:S(2)}, u32[]{:S(2)}) collective-permute-start(bf16[1,128,8192]{2,1,0:T(8,128)(2,1)} %collective-permute-done), channel_id=1, source_target_pairs={{0,1},{1,2},{2,3},{3,4},{4,5},{5,6},{6,7},{7,0},{8,9},{9,10},{10,1... | collective-permute-start | bytes 6291464 | tf_op jit(solution)/shard_map/ppermute | solution.py:71
  102.9 11.6 %copy-start.2 = (bf16[1,1024,512]{2,1,0:T(8,128)(2,1)S(1)}, bf16[1,1024,512]{2,1,0:T(8,128)(2,1)}, u32[]{:S(2)}) copy-start(bf16[1,1024,512]{2,1,0:T(8,128)(2,1)} %param.10) | copy-start | bytes 3145732
  117.3 1.7 copy-start.1
  119.2 79.1 %collective-permute-start.3 = (bf16[1,128,8192]{2,1,0:T(8,128)(2,1)}, bf16[1,128,8192]{2,1,0:T(8,128)(2,1)S(1)}, u32[]{:S(2)}, u32[]{:S(2)}) collective-permute-start(bf16[1,128,8192]{2,1,0:T(8,128)(2,1)} %collective-permute-done.1), channel_id=1, source_target_pairs={{0,7},{1,0},{2,1},{3,2},{4,3},{5,4},{6,5},{7,6},{8,15},{9,8},{10,9... | collective-permute-start | bytes 6291464 | tf_op jit(solution)/shard_map/ppermute | solution.py:81
  192.1 91.1 %collective-permute-start.4 = (bf16[1,128,8192]{2,1,0:T(8,128)(2,1)}, bf16[1,128,8192]{2,1,0:T(8,128)(2,1)S(1)}, u32[]{:S(2)}, u32[]{:S(2)}) collective-permute-start(bf16[1,128,8192]{2,1,0:T(8,128)(2,1)} %collective-permute-done.2), channel_id=1, source_target_pairs={{0,1},{1,2},{2,3},{3,4},{4,5},{5,6},{6,7},{7,0},{8,9},{9,10},{10,1... | collective-permute-start | bytes 6291464 | tf_op jit(solution)/shard_map/ppermute | solution.py:71
  198.3 133.2 %collective-permute-start.5 = (bf16[1,128,8192]{2,1,0:T(8,128)(2,1)S(1)}, bf16[1,128,8192]{2,1,0:T(8,128)(2,1)S(1)}, u32[]{:S(2)}, u32[]{:S(2)}) collective-permute-start(bf16[1,128,8192]{2,1,0:T(8,128)(2,1)S(1)} %collective-permute-done.3), channel_id=1, source_target_pairs={{0,7},{1,0},{2,1},{3,2},{4,3},{5,4},{6,5},{7,6},{8,15},{9,8},{10,9... | collective-permute-start | bytes 6291464 | tf_op jit(solution)/shard_map/ppermute | solution.py:81
  283.2 48.6 %collective-permute-start.6 = (bf16[1,128,8192]{2,1,0:T(8,128)(2,1)S(1)}, bf16[1,128,8192]{2,1,0:T(8,128)(2,1)S(1)}, u32[]{:S(2)}, u32[]{:S(2)}) collective-permute-start(bf16[1,128,8192]{2,1,0:T(8,128)(2,1)S(1)} %collective-permute-done.4), channel_id=1, source_target_pairs={{0,1},{1,2},{2,3},{3,4},{4,5},{5,6},{6,7},{7,0},{8,9},{9,10},{10,1... | collective-permute-start | bytes 6291464 | tf_op jit(solution)/shard_map/ppermute | solution.py:71
  286.1 46.0 %copy-start.4 = (bf16[1,4096,128]{2,1,0:T(8,128)(2,1)S(1)}, bf16[1,4096,128]{2,1,0:T(8,128)(2,1)}, u32[]{:S(2)}) copy-start(bf16[1,4096,128]{2,1,0:T(8,128)(2,1)} %param.9) | copy-start | bytes 3145732
  331.6 1.2 copy-start.5
  335.2 25.3 %collective-permute-start.7 = (f32[1,1024,256]{1,2,0:T(8,128)S(1)}, f32[1,1024,256]{1,2,0:T(8,128)}, u32[]{:S(2)}, u32[]{:S(2)}) collective-permute-start(f32[1,1024,256]{1,2,0:T(8,128)S(1)} %fusion.49), channel_id=1, source_target_pairs={{0,1},{1,0},{2,3},{3,2},{4,5},{5,4},{6,7},{7,6},{8,9},{9,8},{10,11... | collective-permute-start | bytes 3145736 | tf_op jit(solution)/shard_map/ppermute | solution.py:14
  364.8 4.8 %copy-start = (f32[1024,512,4]{1,0,2:T(8,128)}, f32[1024,512,4]{1,0,2:T(8,128)S(1)}, u32[]{:S(2)}) copy-start(f32[1024,512,4]{1,0,2:T(8,128)S(1)} %get-tuple-element.19) | copy-start | bytes 25165828
  364.8 2.0 copy-start.3
  393.4 24.3 %collective-permute-start.8 = (f32[1,1024,256]{1,2,0:T(8,128)S(1)}, f32[1,1024,256]{1,2,0:T(8,128)S(1)}, u32[]{:S(2)}, u32[]{:S(2)}) collective-permute-start(f32[1,1024,256]{1,2,0:T(8,128)S(1)} %fusion.66), channel_id=1, source_target_pairs={{0,1},{1,0},{2,3},{3,2},{4,5},{5,4},{6,7},{7,6},{8,9},{9,8},{10,11... | collective-permute-start | bytes 3145736 | tf_op jit(solution)/shard_map/ppermute | solution.py:14
  424.3 20.8 %reduce-scatter.5.cloned.1.call-start = ((), (), s32[]{:S(2)}) async-start(), calls=%async_computation.3 | async-start | bytes 3145728 | tf_op jit(solution)/shard_map/reduce_scatter | solution.py:151
Sparse Core Ops, SparseCore 0:
  424.4 6.8 reduce-scatter.2
  434.3 10.7 reduce-scatter.4
